TPU v7x, 256 devices: a whole 4x4x8 slice. The times are simulated.
256 devices in a mesh: dp: 8 (over z), seq: 32 (over x, y, core).
Axes of the slice: x: 4, y: 4, z: 8, core: 2. Of those that a mesh axis runs over, the one named last changes fastest.
Arguments:
- values_in: bfloat16 [8, 4096, 2048], P('dp', 'seq'), may hold values from -6 to 6
- input_proj: bfloat16 [8, 4096, 128], P('dp', 'seq'), may hold values from -0.5 to 0.5
- output_proj: bfloat16 [8, 4096, 128], P('dp', 'seq'), may hold values from -0.09375 to 0.09375
- log_decay: float32 [8, 32, 4096], P('dp', None, 'seq'), may hold values from -1 to 0, as said below
- doc_lengths: int32 [8, 8], P('dp'), may hold values from 1 to 2048, 4096 in all within a row
- skip_gain: float32 [32], replicated, may hold values from 0.5 to 1.5
- out_cotangent: bfloat16 [8, 4096, 2048], P('dp', 'seq'), may hold values from -6 to 6
Outputs:
- mixed_out: bfloat16 [8, 4096, 2048], P('dp', 'seq')
- values_grad: bfloat16 [8, 4096, 2048], P('dp', 'seq')
- input_grad: float32 [8, 4096, 128], P('dp', 'seq')
- output_grad: float32 [8, 4096, 128], P('dp', 'seq')
- decay_grad: float32 [8, 32, 4096], P('dp', None, 'seq')
- skip_grad: float32 [32], replicated
Inputs may be any that keep to these rules, and one draw needn't show every extreme that they name: `doc_lengths`: one row lists the documents of one sequence in order and sums to 4096. `log_decay`: negative log decay of each head at each token.
All inputs are finite; a program needn't handle non-finite values.
Results may differ from a plain program's by a relative error of at most 0.0056.
Values sent between devices are 32-bit elements; how exact they have to be, the bound alone decides.
No kernel may reach another device: no remote copies, remote signals or barrier semaphores. Data moves between devices by JAX's collectives and lax.ppermute only.
A program may use at most 128 MiB of HBM per device.

v0:
```python
import functools
import jax
import jax.numpy as jnp
from jax import lax
from jax.sharding import Mesh
from jax.sharding import PartitionSpec as P

SEQ = ("seq_0", "seq_1", "seq_2")
DP_SEQ = ("dp", "seq_0", "seq_1", "seq_2")


def in_one_piece(arrays, axis, split_dim, concat_dim, along):
    ends, at = ([], 0)
    for a in arrays[:-1]:
        at += a.shape[along]
        ends.append(at)
    both = jnp.concatenate(arrays, axis=along)
    return tuple(
        jnp.split(
            lax.all_to_all(both, axis, split_axis=split_dim, concat_axis=concat_dim, tiled=True),
            ends,
            axis=along,
        )
    )


def one_axis_at_a_time(x, axes):
    return functools.reduce(lax.psum, axes, x)


def product(form, left_side, right_side):
    return jnp.einsum(form, left_side, right_side, preferred_element_type=jnp.float32)


def block_stats(log_rows, resets):
    log_cum = jnp.cumsum(log_rows, axis=1)
    seg_count = jnp.cumsum(resets)
    log_end = log_cum[:, -1:]
    count_end = seg_count[-1]
    carry_gain = jnp.exp(log_end[:, 0]) * (count_end == 0).astype(jnp.float32)
    weight_end = jnp.exp(log_end - log_cum) * (seg_count == count_end).astype(jnp.float32)[None, :]
    weight_start = jnp.exp(log_cum) * (seg_count == 0).astype(jnp.float32)[None, :]
    return (log_cum, seg_count, carry_gain, weight_end, weight_start)


def head_scale(values, factors):
    row_count, inner_width = values.shape
    head_count = factors.shape[0]
    shaped = values.reshape(row_count, head_count, inner_width // head_count)
    return (shaped * factors.T[:, :, None]).reshape(row_count, inner_width)


def head_dot(left_side, right_side, head_count):
    row_count = left_side.shape[0]
    joined = left_side.astype(jnp.float32) * right_side.astype(jnp.float32)
    return jnp.sum(joined.reshape(row_count, head_count, -1), axis=2).T


def finish_block(
    values,
    input_rows,
    output_rows,
    grads_in,
    resets,
    skip_gain,
    stats,
    weighted_values,
    weighted_grads,
    state_in,
    adjoint_in,
):
    log_cum, seg_count, carry_gain, weight_end, weight_start = stats
    head_count = log_cum.shape[0]
    row_count, inner_width = values.shape
    head_dim = inner_width // head_count
    state_half = state_in.astype(jnp.bfloat16)
    adjoint_half = adjoint_in.astype(jnp.bfloat16)
    state_read = product("ln,in->li", output_rows, state_half)
    adjoint_read = product("ln,in->li", input_rows, adjoint_half)
    scores = product("tn,sn->ts", output_rows, input_rows)
    position = jnp.arange(row_count, dtype=jnp.int32)
    causal = (position[None, :] <= position[:, None]) & (seg_count[None, :] == seg_count[:, None])
    group_size = min(4, head_count)
    outs_within = []
    outs_back = []
    grad_parts = []
    grad_scores = jnp.zeros((row_count, row_count), jnp.float32)
    for block_index in range(head_count // group_size):
        first_head = block_index * group_size
        low_col = first_head * head_dim
        high_col = (first_head + group_size) * head_dim
        value_group = values[:, low_col:high_col].reshape(row_count, group_size, head_dim)
        grad_group = grads_in[:, low_col:high_col].reshape(row_count, group_size, head_dim)
        log_group = log_cum[first_head : first_head + group_size]
        log_gap = log_group[:, :, None] - log_group[:, None, :]
        decay_mat = jnp.exp(jnp.where(causal[None], log_gap, -jnp.inf))
        weighted = scores[None] * decay_mat
        mix_half = weighted.astype(jnp.bfloat16)
        outs_within.append(product("gts,sgp->tgp", mix_half, value_group).reshape(row_count, -1))
        outs_back.append(product("gts,tgp->sgp", mix_half, grad_group).reshape(row_count, -1))
        grad_mix = product("tgp,sgp->gts", grad_group, value_group)
        sensitivity = grad_mix * weighted
        grad_parts.append(jnp.sum(sensitivity, axis=2) - jnp.sum(sensitivity, axis=1))
        grad_scores = grad_scores + jnp.sum(grad_mix * decay_mat, axis=0)
    within_out = jnp.concatenate(outs_within, axis=1)
    back_part = jnp.concatenate(outs_back, axis=1)
    grad_cum = jnp.concatenate(grad_parts, axis=0)
    skip_rows = jnp.repeat(skip_gain, head_dim)[None, :]
    mixed = (within_out + head_scale(state_read, weight_start) + skip_rows * values).astype(
        jnp.bfloat16
    )
    values_grad = (back_part + head_scale(adjoint_read, weight_end) + skip_rows * grads_in).astype(
        jnp.bfloat16
    )
    grad_start = head_dot(grads_in, state_read, head_count)
    grad_end = head_dot(values, adjoint_read, head_count)
    grad_gain = jnp.sum((state_in * adjoint_in).reshape(head_count, -1), axis=1)
    end_total = jnp.sum(weight_end * grad_end, axis=1) + carry_gain * grad_gain
    grad_cum = grad_cum + weight_start * grad_start - weight_end * grad_end
    grad_cum = grad_cum.at[:, -1].add(end_total)
    decay_raw = (
        jnp.flip(jnp.cumsum(jnp.flip(grad_cum, 1), axis=1), 1)
        * (1 - resets).astype(jnp.float32)[None, :]
    )
    grad_half = grad_scores.astype(jnp.bfloat16)
    input_raw = product("ts,tn->sn", grad_half, output_rows) + product(
        "li,in->ln", weighted_values, adjoint_half
    )
    output_raw = product("ts,sn->tn", grad_half, input_rows) + product(
        "li,in->ln", weighted_grads, state_half
    )
    skip_part = jnp.sum(head_dot(grads_in, values, head_count), axis=1)
    return (mixed, values_grad, input_raw, output_raw, decay_raw, skip_part)


def body(values_in, input_proj, output_proj, log_decay, doc_lengths, skip_gain, out_cotangent):
    values = values_in[0]
    input_rows = input_proj[0]
    output_rows = output_proj[0]
    grads_in = out_cotangent[0]
    log_rows = log_decay[0]
    row_count, inner_width = values.shape
    head_count = log_rows.shape[0]
    head_dim = inner_width // head_count
    state_width = input_rows.shape[1]
    shards = lax.axis_size(SEQ)
    position = lax.axis_index(SEQ) * row_count + jnp.arange(row_count, dtype=jnp.int32)
    lengths = doc_lengths[0]
    starts = jnp.cumsum(lengths) - lengths
    resets = jnp.any(position[:, None] == starts[None, :], axis=1).astype(jnp.int32)
    stats = block_stats(log_rows, resets)
    log_cum, seg_count, carry_gain, weight_end, weight_start = stats
    weighted_values = head_scale(values, weight_end).astype(jnp.bfloat16)
    weighted_grads = head_scale(grads_in, weight_start).astype(jnp.bfloat16)
    local_state = product("li,ln->in", weighted_values, input_rows)
    local_adjoint = product("li,ln->in", weighted_grads, output_rows)
    gain_rows = jnp.broadcast_to(carry_gain[None, :, None, None], (1, head_count, head_dim, 1))
    shaped = (
        local_state.reshape(1, head_count, head_dim, state_width),
        local_adjoint.reshape(1, head_count, head_dim, state_width),
        gain_rows,
    )
    states_all = lax.all_to_all(shaped[0], SEQ, split_axis=1, concat_axis=0, tiled=True)
    adjoints_all = lax.all_to_all(shaped[1], SEQ, split_axis=1, concat_axis=0, tiled=True)
    gains_all = lax.all_to_all(shaped[2], SEQ, split_axis=1, concat_axis=0, tiled=True)
    anchor = jnp.zeros(states_all.shape[1:], jnp.float32)

    def advance(running, element):
        factor, addend = element
        return (factor * running + addend, running)

    unused_a, state_prefix = lax.scan(advance, anchor, (gains_all, states_all))
    unused_b, adjoint_prefix = lax.scan(advance, anchor, (gains_all, adjoints_all), reverse=True)
    state_back, adjoint_back = in_one_piece((state_prefix, adjoint_prefix), SEQ, 0, 1, 2)
    state_in = state_back.reshape(inner_width, state_width)
    adjoint_in = adjoint_back.reshape(inner_width, state_width)
    results = finish_block(
        values,
        input_rows,
        output_rows,
        grads_in,
        resets,
        skip_gain,
        stats,
        weighted_values,
        weighted_grads,
        state_in,
        adjoint_in,
    )
    mixed, values_grad, input_raw, output_raw, decay_raw, skip_part = results
    token_count = shards * row_count
    seq_count = lax.axis_size("dp")
    input_grad = input_raw * (1.0 / jnp.sqrt(jnp.float32(head_count * head_dim)))
    output_grad = output_raw * jnp.sqrt(
        jnp.float32(state_width) / jnp.float32(head_count * head_dim * token_count)
    )
    decay_grad = decay_raw * (1.0 / jnp.sqrt(jnp.float32(head_dim * token_count)))
    skip_total = one_axis_at_a_time(skip_part, DP_SEQ)
    skip_grad = skip_total / jnp.sqrt(jnp.float32(seq_count * token_count * head_dim))
    return (
        mixed[None],
        values_grad[None],
        input_grad[None],
        output_grad[None],
        decay_grad[None],
        skip_grad,
    )


def solution(mesh):
    finer = Mesh(mesh.devices.reshape(mesh.shape["dp"], 4, 4, 2), ("dp", "seq_0", "seq_1", "seq_2"))
    placed = (
        P("dp", SEQ, None),
        P("dp", SEQ, None),
        P("dp", SEQ, None),
        P("dp", None, SEQ),
        P("dp", None),
        P(),
        P("dp", SEQ, None),
    )
    return jax.shard_map(
        body,
        mesh=finer,
        in_specs=placed,
        out_specs=(
            P("dp", SEQ, None),
            P("dp", SEQ, None),
            P("dp", SEQ, None),
            P("dp", SEQ, None),
            P("dp", None, SEQ),
            P(),
        ),
        check_vma=False,
    )
```

profile of v0, /device:TPU:1, one launch (start us, length us, event | category | flops | bytes accessed | tf_op | source)
XLA Modules:
  0.0 180.9 jit_solution(5471237887130458574)
XLA Ops:
  2.3 1.0 reduce_window_sum.31
  5.5 8.6 %all-to-all-start = ((f32[1,32,64,1]{2,3,0,1:T(1,128)}), f32[1,32,64,1]{2,3,0,1:T(1,128)S(1)}, u32[]{:S(2)}, u32[]{:S(2)}) async-start(f32[1,32,64,1]{2,3,0,1:T(1,128)} %broadcast_in_dim.133), calls=%async_computation | async-start | bytes 32768 | tf_op jit(solution)/shard_map/all_to_all | solution.py:165
  15.6 1.3 copy.85
  17.0 1.3 copy.92
  19.5 1.0 fusion.78
  20.8 0.9 fusion.211
  21.7 0.9 fusion.74
  22.9 0.9 fusion.210
  24.4 0.9 fusion.209
  25.9 0.9 fusion.208
  27.2 1.3 convolution_bitcast_fusion.2
  28.7 1.3 convolution_bitcast_fusion.3
  31.7 1.8 fusion.82
  33.7 0.9 copy-done.9
  34.6 7.4 %all-to-all-start.2 = ((f32[1,32,64,128]{3,2,0,1:T(8,128)}), f32[1,32,64,128]{3,2,0,1:T(8,128)S(1)}, u32[]{:S(2)}, u32[]{:S(2)}) async-start(f32[1,32,64,128]{3,2,0,1:T(8,128)} %convolution_bitcast_fusion.2), calls=%async_computation.2 | async-start | bytes 2097152 | tf_op jit(solution)/shard_map/all_to_all | solution.py:164
  42.0 0.9 constant_dynamic-update-slice_fusion.10
  42.9 1.0 copy-done.7
  43.9 1.1 fusion.207
  45.0 1.1 fusion.206
  46.1 1.1 fusion.205
  47.2 3.5 %fusion.52 = (f32[4,128]{1,0:T(4,128)}, f32[4,128]{1,0:T(4,128)}, f32[128,128]{1,0:T(8,128)}, f32[128,128]{1,0:T(8,128)}, f32[4,128]{1,0:T(4,128)}, /*index=5*/f...) fusion(f32[4,128]{1,0:T(4,128)} %get-tuple-element.369, ...), kind=kOutput, calls=%fused_computation.97 | convolution fusion | flops 12443648 | bytes 2621440 | tf_op jit(solution)/shard_map/tgp,sgp->gts/dot_general | solution.py:32
  50.7 8.2 %all-to-all-done.2 = f32[1,32,64,128]{3,2,0,1:T(8,128)S(1)} async-done(((f32[1,32,64,128]{3,2,0,1:T(8,128)}), f32[1,32,64,128]{3,2,0,1:T(8,128)S(1)}, u32[]{:S(2)}, u32[]{:S(2)}) %all-to-all-start.2) | async-done | bytes 1048608 | tf_op jit(solution)/shard_map/all_to_all | solution.py:164
  58.9 4.5 %all-to-all-start.1 = ((f32[1,32,64,128]{3,2,0,1:T(8,128)}), f32[1,32,64,128]{3,2,0,1:T(8,128)}, u32[]{:S(2)}, u32[]{:S(2)}) async-start(f32[1,32,64,128]{3,2,0,1:T(8,128)} %convolution_bitcast_fusion.3), calls=%async_computation.1 | async-start | bytes 2097152 | tf_op jit(solution)/shard_map/all_to_all | solution.py:163
  63.5 3.1 %while.32 = (s32[]{:T(128)}, f32[1,64,128]{2,1,0:T(8,128)S(1)}, f32[32,1,64,128]{3,2,1,0:T(8,128)S(1)}, f32[32,1,64,1]{2,3,1,0:T(1,128)S(1)}, f32[32,1,64,128]{3...) while((s32[]{:T(128)}, f32[1,64,128]{2,1,0:T(8,128)S(1)}, ...), condition=%wide.region_7.8_spmd.clone, body=%wide.region_6.7_spmd.clone.sunk | while | flops 32772 | bytes 164736 | solution.py:173
  66.6 13.7 %all-to-all-done.1 = f32[1,32,64,128]{3,2,0,1:T(8,128)} async-done(((f32[1,32,64,128]{3,2,0,1:T(8,128)}), f32[1,32,64,128]{3,2,0,1:T(8,128)}, u32[]{:S(2)}, u32[]{:S(2)}) %all-to-all-start.1) | async-done | bytes 1048608 | tf_op jit(solution)/shard_map/all_to_all | solution.py:163
  80.4 27.6 %while.31 = (s32[]{:T(128)}, f32[1,64,128]{2,1,0:T(8,128)S(1)}, f32[32,1,64,128]{3,2,1,0:T(8,128)S(1)}, f32[32,1,64,1]{2,3,1,0:T(1,128)S(1)}, f32[32,1,64,128]{3,2,1,0:T(8,128)}, /*index=5*/s32[]{:T(128)}, s32[]{:T(128)}) while((s32[]{:T(128)}, f32[1,64,128]{2,1,0:T(8,128)S(1)}, f32[32,1,64,128]{3,2,1,0:T(8,128)S(1)}, ...), condition=%wide.region_5.6_spmd.clone, body=%wide.region_4.5_spmd.clone.sunk | while | flops 32771 | bytes 164716 | solution.py:172
  80.5 0.8 bitcast_add_fusion.4
  82.2 0.8 bitcast_add_fusion.4
  83.9 0.8 bitcast_add_fusion.4
  84.8 0.8 bitcast_add_fusion.4
  85.7 0.8 bitcast_add_fusion.4
  86.5 0.8 bitcast_add_fusion.4
  108.1 1.5 pad_maximum_fusion
  109.6 4.0 %all-to-all-start.3 = ((f32[32,1,128,128]{3,2,1,0:T(8,128)}), f32[32,1,128,128]{3,2,1,0:T(8,128)S(1)}, u32[]{:S(2)}, u32[]{:S(2)}) async-start(f32[32,1,128,128]{3,2,1,0:T(8,128)} %pad_maximum_fusion), calls=%async_computation.3 | async-start | bytes 4194304 | tf_op jit(solution)/shard_map/all_to_all | solution.py:20
  120.3 17.4 %psum.28 = f32[32]{0:T(128)S(1)} all-reduce(f32[32]{0:T(128)S(1)} %reduce_sum.308), channel_id=1, replica_groups=mesh['dp'=8,'seq_0'=4,'seq_1'=4,'seq_2'=2] {'dp'}, use_global_device_ids=true, to_apply=%region_39.40 | all-reduce | flops 32 | bytes 256 | tf_op jit(solution)/shard_map/psum | solution.py:28
  137.7 8.6 %psum.29 = f32[32]{0:T(128)S(1)} all-reduce(f32[32]{0:T(128)S(1)} %psum.28), channel_id=1, replica_groups=mesh['dp'=8,'seq_0'=4,'seq_1'=4,'seq_2'=2] {'seq_0'}, use_global_device_ids=true, to_apply=%region_40.41 | all-reduce | flops 32 | bytes 256 | tf_op jit(solution)/shard_map/psum | solution.py:28
  146.3 8.4 %psum.30 = f32[32]{0:T(128)S(1)} all-reduce(f32[32]{0:T(128)S(1)} %psum.29), channel_id=1, replica_groups=mesh['dp'=8,'seq_0'=4,'seq_1'=4,'seq_2'=2] {'seq_1'}, use_global_device_ids=true, to_apply=%region_41.42 | all-reduce | flops 32 | bytes 256 | tf_op jit(solution)/shard_map/psum | solution.py:28
  154.7 9.1 %psum.31 = f32[32]{0:T(128)S(1)} all-reduce(f32[32]{0:T(128)S(1)} %psum.30), channel_id=1, replica_groups=mesh['dp'=8,'seq_0'=4,'seq_1'=4,'seq_2'=2] {'seq_2'}, use_global_device_ids=true, to_apply=%region_42.43 | all-reduce | flops 32 | bytes 256 | tf_op jit(solution)/shard_map/psum | solution.py:28
  163.9 1.1 fusion.84
  165.0 1.6 constant_dynamic-update-slice_fusion
  166.6 1.2 fusion.184
  168.3 1.1 add_convert_fusion
  170.4 0.9 multiply_convert_fusion
  171.3 1.0 multiply_convert_fusion.1
  175.5 1.0 copy.105
  176.5 1.0 copy.104
  178.4 1.0 fusion.5
  179.3 1.0 fusion.3
  (344 shorter events, 47.7 us)
Async XLA Ops:
  0.6 18.8 %copy-start = (bf16[1,128,128]{2,1,0:T(8,128)(2,1)S(1)}, bf16[1,128,128]{2,1,0:T(8,128)(2,1)}, u32[]{:S(2)}) copy-start(bf16[1,128,128]{2,1,0:T(8,128)(2,1)} %param.14) | copy-start | bytes 98308
  2.2 1.1 copy-start.35
  5.5 29.1 %all-to-all-start = ((f32[1,32,64,1]{2,3,0,1:T(1,128)}), f32[1,32,64,1]{2,3,0,1:T(1,128)S(1)}, u32[]{:S(2)}, u32[]{:S(2)}) async-start(f32[1,32,64,1]{2,3,0,1:T(1,128)} %broadcast_in_dim.133), calls=%async_computation | async-start | bytes 32768 | tf_op jit(solution)/shard_map/all_to_all | solution.py:165
  14.7 5.8 %copy-start.26 = (f32[4,128]{1,0:T(4,128)}, f32[4,128]{1,0:T(4,128)S(1)}, u32[]{:S(2)}) copy-start(f32[4,128]{1,0:T(4,128)S(1)} %get-tuple-element.370) | copy-start | bytes 6148
  14.7 7.9 %copy-start.27 = (f32[4,128]{1,0:T(4,128)}, f32[4,128]{1,0:T(4,128)S(1)}, u32[]{:S(2)}) copy-start(f32[4,128]{1,0:T(4,128)S(1)} %get-tuple-element.371) | copy-start | bytes 6148
  14.7 9.4 %copy-start.28 = (f32[4,128]{1,0:T(4,128)}, f32[4,128]{1,0:T(4,128)S(1)}, u32[]{:S(2)}) copy-start(f32[4,128]{1,0:T(4,128)S(1)} %get-tuple-element.372) | copy-start | bytes 6148
  14.7 10.9 %copy-start.29 = (f32[4,128]{1,0:T(4,128)}, f32[4,128]{1,0:T(4,128)S(1)}, u32[]{:S(2)}) copy-start(f32[4,128]{1,0:T(4,128)S(1)} %get-tuple-element.373) | copy-start | bytes 6148
  14.7 15.5 %copy-start.30 = (f32[4,128]{1,0:T(4,128)}, f32[4,128]{1,0:T(4,128)S(1)}, u32[]{:S(2)}) copy-start(f32[4,128]{1,0:T(4,128)S(1)} %get-tuple-element.374) | copy-start | bytes 6148
  14.7 16.0 %copy-start.31 = (f32[4,128]{1,0:T(4,128)}, f32[4,128]{1,0:T(4,128)S(1)}, u32[]{:S(2)}) copy-start(f32[4,128]{1,0:T(4,128)S(1)} %get-tuple-element.375) | copy-start | bytes 6148
  14.8 16.6 %copy-start.32 = (f32[4,128]{1,0:T(4,128)}, f32[4,128]{1,0:T(4,128)S(1)}, u32[]{:S(2)}) copy-start(f32[4,128]{1,0:T(4,128)S(1)} %get-tuple-element.376) | copy-start | bytes 6148
  14.8 12.1 %copy-start.21 = (f32[32]{0:T(128)}, f32[32]{0:T(128)S(1)}, u32[]{:S(2)}) copy-start(f32[32]{0:T(128)S(1)} %slice_bitcast_fusion) | copy-start | bytes 388
  17.0 2.4 %copy-start.11 = (bf16[1,128,128]{2,1,0:T(8,128)(2,1)S(1)}, bf16[1,128,128]{2,1,0:T(8,128)(2,1)}, u32[]{:S(2)}) copy-start(bf16[1,128,128]{2,1,0:T(8,128)(2,1)} %param.15) | copy-start | bytes 98308
  18.7 11.2 %copy-start.13 = (bf16[128,256]{0,1:T(8,128)(2,1)}, bf16[128,256]{0,1:T(8,128)(2,1)S(1)}, u32[]{:S(2)}) copy-start(bf16[128,256]{0,1:T(8,128)(2,1)S(1)} %get-tuple-element.354) | copy-start | bytes 196612
  18.7 13.0 %copy-start.19 = (bf16[128,256]{0,1:T(8,128)(2,1)}, bf16[128,256]{0,1:T(8,128)(2,1)S(1)}, u32[]{:S(2)}) copy-start(bf16[128,256]{0,1:T(8,128)(2,1)S(1)} %get-tuple-element.349) | copy-start | bytes 196612
  19.4 10.8 %copy-start.16 = (bf16[128,256]{0,1:T(8,128)(2,1)}, bf16[128,256]{0,1:T(8,128)(2,1)S(1)}, u32[]{:S(2)}) copy-start(bf16[128,256]{0,1:T(8,128)(2,1)S(1)} %get-tuple-element.362) | copy-start | bytes 196612
  19.4 11.4 %copy-start.15 = (bf16[128,256]{0,1:T(8,128)(2,1)}, bf16[128,256]{0,1:T(8,128)(2,1)S(1)}, u32[]{:S(2)}) copy-start(bf16[128,256]{0,1:T(8,128)(2,1)S(1)} %get-tuple-element.363) | copy-start | bytes 196612
  19.4 12.0 %copy-start.14 = (bf16[128,256]{0,1:T(8,128)(2,1)}, bf16[128,256]{0,1:T(8,128)(2,1)S(1)}, u32[]{:S(2)}) copy-start(bf16[128,256]{0,1:T(8,128)(2,1)S(1)} %get-tuple-element.364) | copy-start | bytes 196612
  19.5 11.8 %copy-start.20 = (f32[128,128]{1,0:T(8,128)}, f32[128,128]{1,0:T(8,128)S(1)}, u32[]{:S(2)}) copy-start(f32[128,128]{1,0:T(8,128)S(1)} %fusion.177) | copy-start | bytes 196612
  28.6 3.1 %copy-start.23 = (f32[4,128]{1,0:T(4,128)S(1)}, f32[4,128]{1,0:T(4,128)}, u32[]{:S(2)}) copy-start(f32[4,128]{1,0:T(4,128)} %get-tuple-element.369) | copy-start | bytes 6148
  33.6 1.0 copy-start.9
  34.6 24.3 %all-to-all-start.2 = ((f32[1,32,64,128]{3,2,0,1:T(8,128)}), f32[1,32,64,128]{3,2,0,1:T(8,128)S(1)}, u32[]{:S(2)}, u32[]{:S(2)}) async-start(f32[1,32,64,128]{3,2,0,1:T(8,128)} %convolution_bitcast_fusion.2), calls=%async_computation.2 | async-start | bytes 2097152 | tf_op jit(solution)/shard_map/all_to_all | solution.py:164
  42.9 1.0 copy-start.7
  58.9 21.4 %all-to-all-start.1 = ((f32[1,32,64,128]{3,2,0,1:T(8,128)}), f32[1,32,64,128]{3,2,0,1:T(8,128)}, u32[]{:S(2)}, u32[]{:S(2)}) async-start(f32[1,32,64,128]{3,2,0,1:T(8,128)} %convolution_bitcast_fusion.3), calls=%async_computation.1 | async-start | bytes 2097152 | tf_op jit(solution)/shard_map/all_to_all | solution.py:163
  109.6 4.1 %copy-start.17 = (f32[4,128,64]{1,2,0:T(8,128)S(1)}, f32[4,128,64]{1,2,0:T(8,128)}, u32[]{:S(2)}) copy-start(f32[4,128,64]{1,2,0:T(8,128)} %fusion.78) | copy-start | bytes 393220
  109.6 4.7 %copy-start.34 = (f32[32]{0:T(128)S(1)}, f32[32]{0:T(128)}, u32[]{:S(2)}) copy-start(f32[32]{0:T(128)} %param.18) | copy-start | bytes 388
  109.6 9.8 %copy-start.25 = (f32[4,128]{1,0:T(4,128)S(1)}, f32[4,128]{1,0:T(4,128)}, u32[]{:S(2)}) copy-start(f32[4,128]{1,0:T(4,128)} %get-tuple-element.325) | copy-start | bytes 6148
  109.6 54.3 %copy-start.18 = (bf16[128,256]{0,1:T(8,128)(2,1)S(1)}, bf16[128,256]{0,1:T(8,128)(2,1)}, u32[]{:S(2)}) copy-start(bf16[128,256]{0,1:T(8,128)(2,1)} %get-tuple-element.357) | copy-start | bytes 196612
  109.6 54.3 %copy-start.24 = (f32[4,128]{1,0:T(4,128)S(1)}, f32[4,128]{1,0:T(4,128)}, u32[]{:S(2)}) copy-start(f32[4,128]{1,0:T(4,128)} %get-tuple-element.369) | copy-start | bytes 6148
  109.6 62.7 %all-to-all-start.3 = ((f32[32,1,128,128]{3,2,1,0:T(8,128)}), f32[32,1,128,128]{3,2,1,0:T(8,128)S(1)}, u32[]{:S(2)}, u32[]{:S(2)}) async-start(f32[32,1,128,128]{3,2,1,0:T(8,128)} %pad_maximum_fusion), calls=%async_computation.3 | async-start | bytes 4194304 | tf_op jit(solution)/shard_map/all_to_all | solution.py:20
  172.6 1.5 copy-start.8
  172.6 1.9 %copy-start.10 = (f32[128,2048]{0,1:T(8,128)S(1)}, f32[128,2048]{0,1:T(8,128)}, u32[]{:S(2)}) copy-start(f32[128,2048]{0,1:T(8,128)} %get-tuple-element.384) | copy-start | bytes 3145732
  172.8 0.8 copy-start.1
  172.8 2.4 %copy-start.3 = (bf16[1,32,64,128]{3,2,1,0:T(8,128)(2,1)}, bf16[1,32,64,128]{3,2,1,0:T(8,128)(2,1)S(1)}, u32[]{:S(2)}) copy-start(bf16[1,32,64,128]{3,2,1,0:T(8,128)(2,1)S(1)} %get-tuple-element.347) | copy-start | bytes 1572868
  175.2 2.5 %copy-start.22 = (f32[32]{0:T(128)S(1)}, f32[32]{0:T(128)}, u32[]{:S(2)}) copy-start(f32[32]{0:T(128)} %copy-done.21) | copy-start | bytes 388
  175.3 3.1 %copy-start.4 = (bf16[1,32,64,128]{3,2,1,0:T(8,128)(2,1)S(1)}, bf16[1,32,64,128]{3,2,1,0:T(8,128)(2,1)}, u32[]{:S(2)}) copy-start(bf16[1,32,64,128]{3,2,1,0:T(8,128)(2,1)} %copy-done.3) | copy-start | bytes 1572868
  175.3 3.1 %copy-start.6 = (bf16[128,32,64]{0,2,1:T(8,128)(2,1)S(1)}, bf16[128,32,64]{0,2,1:T(8,128)(2,1)}, u32[]{:S(2)}) copy-start(bf16[128,32,64]{0,2,1:T(8,128)(2,1)} %multiply_convert_fusion.1) | copy-start | bytes 1572868
  175.3 3.1 %copy-start.12 = (f32[128,128]{1,0:T(8,128)S(1)}, f32[128,128]{1,0:T(8,128)}, u32[]{:S(2)}) copy-start(f32[128,128]{1,0:T(8,128)} %fusion.180) | copy-start | bytes 196612
  175.5 3.9 %copy-start.2 = (bf16[1,32,64,128]{3,2,1,0:T(8,128)(2,1)S(1)}, bf16[1,32,64,128]{3,2,1,0:T(8,128)(2,1)}, u32[]{:S(2)}) copy-start(bf16[1,32,64,128]{3,2,1,0:T(8,128)(2,1)} %copy-done.1) | copy-start | bytes 1572868
  175.5 3.8 %copy-start.5 = (bf16[128,32,64]{0,2,1:T(8,128)(2,1)S(1)}, bf16[128,32,64]{0,2,1:T(8,128)(2,1)}, u32[]{:S(2)}) copy-start(bf16[128,32,64]{0,2,1:T(8,128)(2,1)} %multiply_convert_fusion) | copy-start | bytes 1572868
  176.5 3.8 %copy-start.33 = (f32[128]{0:T(128)S(1)}, f32[128]{0:T(128)}, u32[]{:S(2)}) copy-start(f32[128]{0:T(128)} %fusion.184) | copy-start | bytes 1540
where the time goes:
time: 184 us; the launch traced here: 181 us
  other arithmetic  47.6 us (26%)
  blocking collectives  43.6 us (24%)
  matrix products  25.2 us (14%)
  starting transfers between devices  24.5 us (13%)
  waiting for transfers between devices  22 us (12%)
  local copies, waits for them, and re-layouts  15.6 us (8%)
  between operations  1.95 us (1%)
    psum x4, blocking collectives, one_axis_at_a_time(): return functools.reduce(lax.psum, axes, x)  43.6 us
    add x64, other arithmetic, advance(): return (factor * running + addend, running)  29.5 us
    dot_general x33, matrix products, product(): jnp.einsum(form, left_side, right_side, preferred_element_type=jnp.float32)  25.2 us
    all_to_all x1, waiting for transfers between devices, body(): lax.all_to_all(shaped[0], SEQ, split_axis=1, concat_axis=0, tiled=True)  13.7 us
    unnamed x90, local copies, waits for them, and re-layouts  9.78 us
    all_to_all x1, starting transfers between devices, body(): lax.all_to_all(shaped[2], SEQ, split_axis=1, concat_axis=0, tiled=True)  8.58 us
    all_to_all x1, waiting for transfers between devices, body(): lax.all_to_all(shaped[1], SEQ, split_axis=1, concat_axis=0, tiled=True)  8.21 us
    all_to_all x1, starting transfers between devices, body(): lax.all_to_all(shaped[1], SEQ, split_axis=1, concat_axis=0, tiled=True)  7.4 us
  transfers between devices with their start and end apart: 4, of which 2 were waited for; matrix products, arithmetic and copies ran while one was open for 25% of the time, Pallas kernels for 0%

commit v1 on v0

--- a/solution.py
+++ b/solution.py
@@ -161,7 +161,10 @@
         gain_rows,
     )
     states_all = lax.all_to_all(shaped[0], SEQ, split_axis=1, concat_axis=0, tiled=True)
-    adjoints_all = lax.all_to_all(shaped[1], SEQ, split_axis=1, concat_axis=0, tiled=True)
+    adjoints_all = jnp.concatenate(
+        lax.all_to_all(jnp.stack(jnp.split(shaped[1], lax.axis_size(SEQ), axis=1)), SEQ, 0, 0),
+        axis=0,
+    )
     gains_all = lax.all_to_all(shaped[2], SEQ, split_axis=1, concat_axis=0, tiled=True)
     anchor = jnp.zeros(states_all.shape[1:], jnp.float32)
 

time: 184 us -> 188 us (1.022)
  matrix products: 25.2 us -> 27.2 us
    dot_general x33, matrix products: 25.2 us -> 27.2 us  [product(): jnp.einsum(form, left_side, right_side, preferred_element_type=jnp.float32)]
    unnamed x90 -> x137, local copies, waits for them, and re-layouts: 9.78 us -> 10.8 us
where the time goes in v1:
time: 188 us; the launch traced here: 185 us
  other arithmetic  47.6 us (25%)
  blocking collectives  43.7 us (23%)
  matrix products  27.2 us (14%)
  starting transfers between devices  24.5 us (13%)
  waiting for transfers between devices  21.9 us (12%)
  local copies, waits for them, and re-layouts  16.6 us (9%)
  between operations  2.29 us (1%)
    psum x4, blocking collectives, one_axis_at_a_time(): return functools.reduce(lax.psum, axes, x)  43.7 us
    add x64, other arithmetic, advance(): return (factor * running + addend, running)  29.5 us
    dot_general x33, matrix products, product(): jnp.einsum(form, left_side, right_side, preferred_element_type=jnp.float32)  27.2 us
    all_to_all x1, waiting for transfers between devices, body(): lax.all_to_all(shaped[0], SEQ, split_axis=1, concat_axis=0, tiled=True)  13.7 us
    unnamed x137, local copies, waits for them, and re-layouts  10.8 us
    all_to_all x1, starting transfers between devices, body(): lax.all_to_all(shaped[2], SEQ, split_axis=1, concat_axis=0, tiled=True)  8.58 us
    all_to_all x1, waiting for transfers between devices, body(): lax.all_to_all(jnp.stack(jnp.split(shaped[1], lax.axis_size(SEQ), axis=1)...  8.19 us
    all_to_all x1, starting transfers between devices, body(): lax.all_to_all(jnp.stack(jnp.split(shaped[1], lax.axis_size(SEQ), axis=1)...  7.41 us
  transfers between devices with their start and end apart: 4, of which 2 were waited for; matrix products, arithmetic and copies ran while one was open for 25% of the time, Pallas kernels for 0%

profile of v1, /device:TPU:1, one launch (start us, length us, event | category | flops | bytes accessed | tf_op | source)
XLA Modules:
  0.0 184.5 jit_solution(3556942553266807134)
XLA Ops:
  2.8 1.0 reduce_window_sum.31
  6.1 8.6 %all-to-all-start = ((f32[1,32,64,1]{2,3,0,1:T(1,128)}), f32[1,32,64,1]{2,3,0,1:T(1,128)S(1)}, u32[]{:S(2)}, u32[]{:S(2)}) async-start(f32[1,32,64,1]{2,3,0,1:T(1,128)} %broadcast_in_dim.133), calls=%async_computation | async-start | bytes 32768 | tf_op jit(solution)/shard_map/all_to_all | solution.py:168
  16.2 1.3 copy.82
  17.6 1.3 copy.89
  20.1 1.0 fusion.78
  21.1 0.9 fusion.80
  22.0 0.9 fusion.211
  22.9 0.9 fusion.74
  23.9 0.9 fusion.76
  24.8 0.9 fusion.210
  25.7 0.9 fusion.70
  26.6 0.9 fusion.72
  27.6 0.9 fusion.209
  28.5 0.9 fusion.66
  29.4 0.9 fusion.68
  30.3 0.9 fusion.208
  32.0 1.3 convolution_bitcast_fusion.3
  35.9 0.9 fusion.82
  37.1 0.9 copy-done.9
  38.0 7.4 %all-to-all-start.2 = ((f32[32,1,1,64,128]{4,3,2,1,0:T(8,128)}), f32[32,1,1,64,128]{4,3,2,1,0:T(8,128)S(1)}, u32[]{:S(2)}, u32[]{:S(2)}) async-start(f32[32,1,1,64,128]{4,3,2,1,0:T(8,128)} %copy-done.11), calls=%async_computation.2 | async-start | bytes 2097152 | tf_op jit(solution)/shard_map/all_to_all | solution.py:165
  45.4 0.9 constant_dynamic-update-slice_fusion.42
  46.3 1.0 copy-done.7
  47.3 1.1 fusion.207
  48.4 1.1 fusion.206
  49.5 1.1 fusion.205
  50.6 3.5 %fusion.52 = (f32[4,128]{1,0:T(4,128)}, f32[4,128]{1,0:T(4,128)}, f32[128,128]{1,0:T(8,128)}, f32[128,128]{1,0:T(8,128)}, f32[4,128]{1,0:T(4,128)}, /*index=5*/f...) fusion(f32[4,128]{1,0:T(4,128)} %get-tuple-element.369, ...), kind=kOutput, calls=%fused_computation.97 | convolution fusion | flops 12443648 | bytes 2621440 | tf_op jit(solution)/shard_map/tgp,sgp->gts/dot_general | solution.py:32
  54.1 8.2 %all-to-all-done.2 = f32[32,1,1,64,128]{4,3,2,1,0:T(8,128)S(1)} async-done(((f32[32,1,1,64,128]{4,3,2,1,0:T(8,128)}), f32[32,1,1,64,128]{4,3,2,1,0:T(8,128)S(1)}, u32[]{:S(2)}, u32[]{:S(2)}) %all-to-all-start.2) | async-done | bytes 1048608 | tf_op jit(solution)/shard_map/all_to_all | solution.py:165
  62.3 4.5 %all-to-all-start.1 = ((f32[1,32,64,128]{3,2,0,1:T(8,128)}), f32[1,32,64,128]{3,2,0,1:T(8,128)}, u32[]{:S(2)}, u32[]{:S(2)}) async-start(f32[1,32,64,128]{3,2,0,1:T(8,128)} %convolution_bitcast_fusion.3), calls=%async_computation.1 | async-start | bytes 2097152 | tf_op jit(solution)/shard_map/all_to_all | solution.py:163
  66.9 3.1 %while.32 = (s32[]{:T(128)}, f32[1,64,128]{2,1,0:T(8,128)S(1)}, f32[32,1,64,128]{3,2,1,0:T(8,128)S(1)}, f32[32,1,64,1]{2,3,1,0:T(1,128)S(1)}, f32[32,1,64,128]{3...) while((s32[]{:T(128)}, f32[1,64,128]{2,1,0:T(8,128)S(1)}, ...), condition=%wide.region_7.8_spmd.clone, body=%wide.region_6.7_spmd.clone.sunk | while | flops 32772 | bytes 164736 | solution.py:176
  70.0 13.7 %all-to-all-done.1 = f32[1,32,64,128]{3,2,0,1:T(8,128)} async-done(((f32[1,32,64,128]{3,2,0,1:T(8,128)}), f32[1,32,64,128]{3,2,0,1:T(8,128)}, u32[]{:S(2)}, u32[]{:S(2)}) %all-to-all-start.1) | async-done | bytes 1048608 | tf_op jit(solution)/shard_map/all_to_all | solution.py:163
  83.9 27.6 %while.31 = (s32[]{:T(128)}, f32[1,64,128]{2,1,0:T(8,128)S(1)}, f32[32,1,64,128]{3,2,1,0:T(8,128)S(1)}, f32[32,1,64,1]{2,3,1,0:T(1,128)S(1)}, f32[32,1,64,128]{3,2,1,0:T(8,128)}, /*index=5*/s32[]{:T(128)}, s32[]{:T(128)}) while((s32[]{:T(128)}, f32[1,64,128]{2,1,0:T(8,128)S(1)}, f32[32,1,64,128]{3,2,1,0:T(8,128)S(1)}, ...), condition=%wide.region_5.6_spmd.clone, body=%wide.region_4.5_spmd.clone.sunk | while | flops 32771 | bytes 164716 | solution.py:175
  84.8 0.8 bitcast_add_fusion.4
  111.5 1.5 pad_maximum_fusion
  113.0 4.0 %all-to-all-start.3 = ((f32[32,1,128,128]{3,2,1,0:T(8,128)}), f32[32,1,128,128]{3,2,1,0:T(8,128)S(1)}, u32[]{:S(2)}, u32[]{:S(2)}) async-start(f32[32,1,128,128]{3,2,1,0:T(8,128)} %pad_maximum_fusion), calls=%async_computation.3 | async-start | bytes 4194304 | tf_op jit(solution)/shard_map/all_to_all | solution.py:20
  123.7 17.4 %psum.28 = f32[32]{0:T(128)S(1)} all-reduce(f32[32]{0:T(128)S(1)} %reduce_sum.308), channel_id=1, replica_groups=mesh['dp'=8,'seq_0'=4,'seq_1'=4,'seq_2'=2] {'dp'}, use_global_device_ids=true, to_apply=%region_39.40 | all-reduce | flops 32 | bytes 256 | tf_op jit(solution)/shard_map/psum | solution.py:28
  141.1 8.6 %psum.29 = f32[32]{0:T(128)S(1)} all-reduce(f32[32]{0:T(128)S(1)} %psum.28), channel_id=1, replica_groups=mesh['dp'=8,'seq_0'=4,'seq_1'=4,'seq_2'=2] {'seq_0'}, use_global_device_ids=true, to_apply=%region_40.41 | all-reduce | flops 32 | bytes 256 | tf_op jit(solution)/shard_map/psum | solution.py:28
  149.7 8.4 %psum.30 = f32[32]{0:T(128)S(1)} all-reduce(f32[32]{0:T(128)S(1)} %psum.29), channel_id=1, replica_groups=mesh['dp'=8,'seq_0'=4,'seq_1'=4,'seq_2'=2] {'seq_1'}, use_global_device_ids=true, to_apply=%region_41.42 | all-reduce | flops 32 | bytes 256 | tf_op jit(solution)/shard_map/psum | solution.py:28
  158.1 9.3 %psum.31 = f32[32]{0:T(128)S(1)} all-reduce(f32[32]{0:T(128)S(1)} %psum.30), channel_id=1, replica_groups=mesh['dp'=8,'seq_0'=4,'seq_1'=4,'seq_2'=2] {'seq_2'}, use_global_device_ids=true, to_apply=%region_42.43 | all-reduce | flops 32 | bytes 256 | tf_op jit(solution)/shard_map/psum | solution.py:28
  167.4 1.1 fusion.84
  168.6 1.6 constant_dynamic-update-slice_fusion
  170.2 1.2 fusion.184
  171.9 1.1 add_convert_fusion
  173.9 0.9 multiply_convert_fusion
  174.9 1.0 multiply_convert_fusion.1
  179.1 1.0 copy.101
  180.1 1.0 copy.100
  181.9 1.0 fusion.5
  182.9 1.0 fusion.3
  (392 shorter events, 51.7 us)
Async XLA Ops:
  0.6 19.3 %copy-start = (bf16[1,128,128]{2,1,0:T(8,128)(2,1)S(1)}, bf16[1,128,128]{2,1,0:T(8,128)(2,1)}, u32[]{:S(2)}) copy-start(bf16[1,128,128]{2,1,0:T(8,128)(2,1)} %param.14) | copy-start | bytes 98308
  2.2 0.6 copy-start.43
  6.1 31.9 %all-to-all-start = ((f32[1,32,64,1]{2,3,0,1:T(1,128)}), f32[1,32,64,1]{2,3,0,1:T(1,128)S(1)}, u32[]{:S(2)}, u32[]{:S(2)}) async-start(f32[1,32,64,1]{2,3,0,1:T(1,128)} %broadcast_in_dim.133), calls=%async_computation | async-start | bytes 32768 | tf_op jit(solution)/shard_map/all_to_all | solution.py:168
  15.3 5.8 %copy-start.33 = (f32[4,128]{1,0:T(4,128)}, f32[4,128]{1,0:T(4,128)S(1)}, u32[]{:S(2)}) copy-start(f32[4,128]{1,0:T(4,128)S(1)} %get-tuple-element.370) | copy-start | bytes 6148
  15.3 8.6 %copy-start.34 = (f32[4,128]{1,0:T(4,128)}, f32[4,128]{1,0:T(4,128)S(1)}, u32[]{:S(2)}) copy-start(f32[4,128]{1,0:T(4,128)S(1)} %get-tuple-element.371) | copy-start | bytes 6148
  15.3 11.3 %copy-start.35 = (f32[4,128]{1,0:T(4,128)}, f32[4,128]{1,0:T(4,128)S(1)}, u32[]{:S(2)}) copy-start(f32[4,128]{1,0:T(4,128)S(1)} %get-tuple-element.372) | copy-start | bytes 6148
  15.3 14.1 %copy-start.36 = (f32[4,128]{1,0:T(4,128)}, f32[4,128]{1,0:T(4,128)S(1)}, u32[]{:S(2)}) copy-start(f32[4,128]{1,0:T(4,128)S(1)} %get-tuple-element.373) | copy-start | bytes 6148
  15.3 18.3 %copy-start.37 = (f32[4,128]{1,0:T(4,128)}, f32[4,128]{1,0:T(4,128)S(1)}, u32[]{:S(2)}) copy-start(f32[4,128]{1,0:T(4,128)S(1)} %get-tuple-element.374) | copy-start | bytes 6148
  15.3 18.8 %copy-start.38 = (f32[4,128]{1,0:T(4,128)}, f32[4,128]{1,0:T(4,128)S(1)}, u32[]{:S(2)}) copy-start(f32[4,128]{1,0:T(4,128)S(1)} %get-tuple-element.375) | copy-start | bytes 6148
  15.3 19.4 %copy-start.39 = (f32[4,128]{1,0:T(4,128)}, f32[4,128]{1,0:T(4,128)S(1)}, u32[]{:S(2)}) copy-start(f32[4,128]{1,0:T(4,128)S(1)} %get-tuple-element.376) | copy-start | bytes 6148
  15.3 15.9 %copy-start.29 = (f32[32]{0:T(128)}, f32[32]{0:T(128)S(1)}, u32[]{:S(2)}) copy-start(f32[32]{0:T(128)S(1)} %slice_bitcast_fusion.32) | copy-start | bytes 388
  17.5 2.4 %copy-start.12 = (bf16[1,128,128]{2,1,0:T(8,128)(2,1)S(1)}, bf16[1,128,128]{2,1,0:T(8,128)(2,1)}, u32[]{:S(2)}) copy-start(bf16[1,128,128]{2,1,0:T(8,128)(2,1)} %param.15) | copy-start | bytes 98308
  19.3 14.0 %copy-start.14 = (bf16[128,256]{0,1:T(8,128)(2,1)}, bf16[128,256]{0,1:T(8,128)(2,1)S(1)}, u32[]{:S(2)}) copy-start(bf16[128,256]{0,1:T(8,128)(2,1)S(1)} %get-tuple-element.354) | copy-start | bytes 196612
  19.3 16.3 %copy-start.26 = (bf16[128,256]{0,1:T(8,128)(2,1)}, bf16[128,256]{0,1:T(8,128)(2,1)S(1)}, u32[]{:S(2)}) copy-start(bf16[128,256]{0,1:T(8,128)(2,1)S(1)} %get-tuple-element.349) | copy-start | bytes 196612
  20.0 13.6 %copy-start.17 = (bf16[128,256]{0,1:T(8,128)(2,1)}, bf16[128,256]{0,1:T(8,128)(2,1)S(1)}, u32[]{:S(2)}) copy-start(bf16[128,256]{0,1:T(8,128)(2,1)S(1)} %get-tuple-element.362) | copy-start | bytes 196612
  20.0 14.2 %copy-start.16 = (bf16[128,256]{0,1:T(8,128)(2,1)}, bf16[128,256]{0,1:T(8,128)(2,1)S(1)}, u32[]{:S(2)}) copy-start(bf16[128,256]{0,1:T(8,128)(2,1)S(1)} %get-tuple-element.363) | copy-start | bytes 196612
  20.0 14.8 %copy-start.15 = (bf16[128,256]{0,1:T(8,128)(2,1)}, bf16[128,256]{0,1:T(8,128)(2,1)S(1)}, u32[]{:S(2)}) copy-start(bf16[128,256]{0,1:T(8,128)(2,1)S(1)} %get-tuple-element.364) | copy-start | bytes 196612
  20.1 14.6 %copy-start.27 = (f32[128,128]{1,0:T(8,128)}, f32[128,128]{1,0:T(8,128)S(1)}, u32[]{:S(2)}) copy-start(f32[128,128]{1,0:T(8,128)S(1)} %fusion.177) | copy-start | bytes 196612
  33.9 1.7 copy-start.31
  34.7 2.1 %copy-start.24 = (f32[4,128,64]{1,2,0:T(8,128)S(1)}, f32[4,128,64]{1,2,0:T(8,128)}, u32[]{:S(2)}) copy-start(f32[4,128,64]{1,2,0:T(8,128)} %fusion.68) | copy-start | bytes 393220
  34.8 2.1 %copy-start.23 = (f32[4,128,64]{1,2,0:T(8,128)S(1)}, f32[4,128,64]{1,2,0:T(8,128)}, u32[]{:S(2)}) copy-start(f32[4,128,64]{1,2,0:T(8,128)} %fusion.72) | copy-start | bytes 393220
  35.0 0.8 copy-start.28
  35.1 1.9 %copy-start.22 = (f32[4,128,64]{1,2,0:T(8,128)S(1)}, f32[4,128,64]{1,2,0:T(8,128)}, u32[]{:S(2)}) copy-start(f32[4,128,64]{1,2,0:T(8,128)} %fusion.76) | copy-start | bytes 393220
  35.1 1.9 %copy-start.20 = (f32[4,128,64]{1,2,0:T(8,128)S(1)}, f32[4,128,64]{1,2,0:T(8,128)}, u32[]{:S(2)}) copy-start(f32[4,128,64]{1,2,0:T(8,128)} %fusion.80) | copy-start | bytes 393220
  35.2 1.8 copy-start.21
  35.3 2.7 %copy-start.19 = (f32[4,128,64]{1,2,0:T(8,128)S(1)}, f32[4,128,64]{1,2,0:T(8,128)}, u32[]{:S(2)}) copy-start(f32[4,128,64]{1,2,0:T(8,128)} %fusion.70) | copy-start | bytes 393220
  35.5 2.4 %copy-start.11 = (f32[32,1,1,64,128]{4,3,2,1,0:T(8,128)}, f32[32,1,1,64,128]{4,3,2,1,0:T(8,128)S(1)}, u32[]{:S(2)}) copy-start(f32[32,1,1,64,128]{4,3,2,1,0:T(8,128)S(1)} %constant_dynamic-update-slice_fusion.8) | copy-start | bytes 3145732
  37.0 1.0 copy-start.9
  38.0 24.3 %all-to-all-start.2 = ((f32[32,1,1,64,128]{4,3,2,1,0:T(8,128)}), f32[32,1,1,64,128]{4,3,2,1,0:T(8,128)S(1)}, u32[]{:S(2)}, u32[]{:S(2)}) async-start(f32[32,1,1,64,128]{4,3,2,1,0:T(8,128)} %copy-done.11), calls=%async_computation.2 | async-start | bytes 2097152 | tf_op jit(solution)/shard_map/all_to_all | solution.py:165
  46.3 1.0 copy-start.7
  62.3 21.4 %all-to-all-start.1 = ((f32[1,32,64,128]{3,2,0,1:T(8,128)}), f32[1,32,64,128]{3,2,0,1:T(8,128)}, u32[]{:S(2)}, u32[]{:S(2)}) async-start(f32[1,32,64,128]{3,2,0,1:T(8,128)} %convolution_bitcast_fusion.3), calls=%async_computation.1 | async-start | bytes 2097152 | tf_op jit(solution)/shard_map/all_to_all | solution.py:163
  113.0 4.1 %copy-start.18 = (f32[4,128,64]{1,2,0:T(8,128)S(1)}, f32[4,128,64]{1,2,0:T(8,128)}, u32[]{:S(2)}) copy-start(f32[4,128,64]{1,2,0:T(8,128)} %fusion.78) | copy-start | bytes 393220
  113.0 4.7 %copy-start.42 = (f32[32]{0:T(128)S(1)}, f32[32]{0:T(128)}, u32[]{:S(2)}) copy-start(f32[32]{0:T(128)} %param.18) | copy-start | bytes 388
  113.0 9.8 %copy-start.40 = (f32[4,128]{1,0:T(4,128)S(1)}, f32[4,128]{1,0:T(4,128)}, u32[]{:S(2)}) copy-start(f32[4,128]{1,0:T(4,128)} %get-tuple-element.325) | copy-start | bytes 6148
  113.0 54.5 %copy-start.25 = (bf16[128,256]{0,1:T(8,128)(2,1)S(1)}, bf16[128,256]{0,1:T(8,128)(2,1)}, u32[]{:S(2)}) copy-start(bf16[128,256]{0,1:T(8,128)(2,1)} %get-tuple-element.357) | copy-start | bytes 196612
  113.0 54.5 %copy-start.32 = (f32[4,128]{1,0:T(4,128)S(1)}, f32[4,128]{1,0:T(4,128)}, u32[]{:S(2)}) copy-start(f32[4,128]{1,0:T(4,128)} %get-tuple-element.369) | copy-start | bytes 6148
  113.0 62.8 %all-to-all-start.3 = ((f32[32,1,128,128]{3,2,1,0:T(8,128)}), f32[32,1,128,128]{3,2,1,0:T(8,128)S(1)}, u32[]{:S(2)}, u32[]{:S(2)}) async-start(f32[32,1,128,128]{3,2,1,0:T(8,128)} %pad_maximum_fusion), calls=%async_computation.3 | async-start | bytes 4194304 | tf_op jit(solution)/shard_map/all_to_all | solution.py:20
  176.2 1.5 copy-start.8
  176.2 1.9 %copy-start.10 = (f32[128,2048]{0,1:T(8,128)S(1)}, f32[128,2048]{0,1:T(8,128)}, u32[]{:S(2)}) copy-start(f32[128,2048]{0,1:T(8,128)} %get-tuple-element.384) | copy-start | bytes 3145732
  176.4 0.8 copy-start.1
  176.4 2.4 %copy-start.3 = (bf16[1,32,64,128]{3,2,1,0:T(8,128)(2,1)}, bf16[1,32,64,128]{3,2,1,0:T(8,128)(2,1)S(1)}, u32[]{:S(2)}) copy-start(bf16[1,32,64,128]{3,2,1,0:T(8,128)(2,1)S(1)} %get-tuple-element.347) | copy-start | bytes 1572868
  178.8 2.5 %copy-start.30 = (f32[32]{0:T(128)S(1)}, f32[32]{0:T(128)}, u32[]{:S(2)}) copy-start(f32[32]{0:T(128)} %copy-done.29) | copy-start | bytes 388
  178.8 3.1 %copy-start.4 = (bf16[1,32,64,128]{3,2,1,0:T(8,128)(2,1)S(1)}, bf16[1,32,64,128]{3,2,1,0:T(8,128)(2,1)}, u32[]{:S(2)}) copy-start(bf16[1,32,64,128]{3,2,1,0:T(8,128)(2,1)} %copy-done.3) | copy-start | bytes 1572868
  178.8 3.1 %copy-start.6 = (bf16[128,32,64]{0,2,1:T(8,128)(2,1)S(1)}, bf16[128,32,64]{0,2,1:T(8,128)(2,1)}, u32[]{:S(2)}) copy-start(bf16[128,32,64]{0,2,1:T(8,128)(2,1)} %multiply_convert_fusion.1) | copy-start | bytes 1572868
  178.8 3.1 %copy-start.13 = (f32[128,128]{1,0:T(8,128)S(1)}, f32[128,128]{1,0:T(8,128)}, u32[]{:S(2)}) copy-start(f32[128,128]{1,0:T(8,128)} %fusion.180) | copy-start | bytes 196612
  179.1 3.9 %copy-start.2 = (bf16[1,32,64,128]{3,2,1,0:T(8,128)(2,1)S(1)}, bf16[1,32,64,128]{3,2,1,0:T(8,128)(2,1)}, u32[]{:S(2)}) copy-start(bf16[1,32,64,128]{3,2,1,0:T(8,128)(2,1)} %copy-done.1) | copy-start | bytes 1572868
  179.1 3.8 %copy-start.5 = (bf16[128,32,64]{0,2,1:T(8,128)(2,1)S(1)}, bf16[128,32,64]{0,2,1:T(8,128)(2,1)}, u32[]{:S(2)}) copy-start(bf16[128,32,64]{0,2,1:T(8,128)(2,1)} %multiply_convert_fusion) | copy-start | bytes 1572868
  180.1 3.8 %copy-start.41 = (f32[128]{0:T(128)S(1)}, f32[128]{0:T(128)}, u32[]{:S(2)}) copy-start(f32[128]{0:T(128)} %fusion.184) | copy-start | bytes 1540
